TPU v7x, 128 devices: a whole 4x4x4 slice. The times are simulated.
128 devices in a mesh: group: 8 (over y, core), tile: 16 (over x, z).
Axes of the slice: x: 4, y: 4, z: 4, core: 2. Of those that a mesh axis runs over, the one named last changes fastest.
Arguments:
- embeddings: bfloat16 [49152, 768], P(('group', 'tile')), may hold values from -15 to 15
- clusters: int32 [49152], P(('group', 'tile')), may hold values from 0 to 31, as said below
- cluster_owner: int32 [32], replicated, may hold values from 0 to 7, as said below
Outputs:
- neighbours: bfloat16 [49152, 768], P(('group', 'tile'))
- log_mass: float32 [49152], P(('group', 'tile'))
Inputs may be any that keep to these rules, and one draw needn't show every extreme that they name: Among the 384 rows of one device at most 72 belong to clusters of any one group; in every draw one group has exactly 72 rows on every device. `cluster_owner`: each group owns exactly 4 clusters.
All inputs are finite; a program needn't handle non-finite values.
Results may differ from a plain program's by a relative error of at most 0.034.
Values may be sent and summed in bfloat16 or wider, within the bound.
No kernel may reach another device: no remote copies, remote signals or barrier semaphores. Data moves between devices by JAX's collectives and lax.ppermute only.
A program may use at most 128 MiB of HBM per device.

v0:
```python
import math
import jax
import jax.numpy as jnp
from jax import lax
from jax.sharding import PartitionSpec as P

score_scale = 3.0
penalty = 2.0


def block_scores(queries, query_ids, key_rows, key_ids):
    feature_width = queries.shape[1]
    products = lax.dot_general(
        queries, key_rows, (((1,), (1,)), ((), ())), preferred_element_type=jnp.float32
    )
    differs = (query_ids[:, None] != key_ids[None, :]).astype(jnp.float32)
    return products * (score_scale / math.sqrt(feature_width)) - penalty * differs


def partial_terms(scores, usable, key_rows):
    row_peak = jnp.max(jnp.where(usable, scores, 0.0), axis=1)
    weights = jnp.exp(jnp.where(usable, scores - row_peak[:, None], -jnp.inf))
    row_total = jnp.sum(weights, axis=1)
    weighted = jnp.dot(weights.astype(jnp.bfloat16), key_rows, preferred_element_type=jnp.float32)
    return (row_peak, row_total, weighted)


def combine_terms(former, second):
    row_peak = jnp.maximum(former[0], second[0])
    factor_one = jnp.exp(former[0] - row_peak)
    factor_two = jnp.exp(second[0] - row_peak)
    row_total = former[1] * factor_one + second[1] * factor_two
    weighted = second[2] * factor_two[:, None]
    return (row_peak, row_total, weighted)


def per_device(embeddings, clusters, cluster_owner):
    row_count = embeddings.shape[0]
    feature_width = embeddings.shape[1]
    groups_total = lax.axis_size("group")
    capacity = 3 * row_count // (2 * groups_total)
    slot_count = groups_total * capacity
    cluster_total = cluster_owner.shape[0]
    table_hit = clusters[:, None] == jnp.arange(cluster_total, dtype=jnp.int32)[None, :]
    group_of = jnp.sum(jnp.where(table_hit, cluster_owner[None, :], 0), axis=1)
    same_group = group_of[:, None] == group_of[None, :]
    row_index = jnp.arange(row_count, dtype=jnp.int32)
    earlier = row_index[None, :] < row_index[:, None]
    rank_in = jnp.sum(same_group & earlier, axis=1)
    slot_of = group_of * capacity + rank_in
    slot_index = jnp.arange(slot_count, dtype=jnp.int32)
    placing = slot_index[:, None] == slot_of[None, :]
    outgoing = jnp.dot(
        placing.astype(jnp.bfloat16), embeddings, preferred_element_type=jnp.float32
    ).astype(jnp.bfloat16)
    outgoing_ids = jnp.sum(jnp.where(placing, clusters[None, :] + 1, 0), axis=1) - 1
    arrived, arrived_ids = (
        lax.all_to_all(
            outgoing.reshape(groups_total, capacity, feature_width),
            "group",
            split_axis=0,
            concat_axis=0,
            tiled=True,
        ),
        lax.all_to_all(
            outgoing_ids.reshape(groups_total, capacity),
            "group",
            split_axis=0,
            concat_axis=0,
            tiled=True,
        ),
    )
    queries = arrived.reshape(slot_count, feature_width)
    query_ids = arrived_ids.reshape(slot_count)
    start_state = (
        jnp.zeros((slot_count,), jnp.float32),
        jnp.ones((slot_count,), jnp.float32),
        jnp.zeros((slot_count, feature_width), jnp.float32),
    )
    tile_pos = lax.axis_index("tile")
    query_pos = tile_pos * slot_count + jnp.arange(slot_count, dtype=jnp.int32)
    key_rows = lax.all_gather(queries, "tile", axis=0, tiled=True)
    key_ids = lax.all_gather(query_ids, "tile", axis=0, tiled=True)
    key_pos = jnp.arange(key_rows.shape[0], dtype=jnp.int32)
    scores = block_scores(queries, query_ids, key_rows, key_ids)
    usable = (key_ids[None, :] >= 0) & (key_pos[None, :] != query_pos[:, None])
    partials = combine_terms(start_state, partial_terms(scores, usable, key_rows))
    row_peak, row_total, weighted = partials
    lse_slots = row_peak + jnp.log(row_total)
    neighbour_slots = (weighted / row_total[:, None]).astype(jnp.bfloat16)
    back_rows, back_lse = (
        lax.all_to_all(
            neighbour_slots.reshape(groups_total, capacity, feature_width),
            "group",
            split_axis=0,
            concat_axis=0,
            tiled=True,
        ),
        lax.all_to_all(
            lse_slots.reshape(groups_total, capacity).astype(jnp.bfloat16),
            "group",
            split_axis=0,
            concat_axis=0,
            tiled=True,
        ).astype(jnp.float32),
    )
    flat_rows = back_rows.reshape(slot_count, feature_width)
    neighbours = jnp.take(flat_rows, slot_of, axis=0)
    log_mass = jnp.take(back_lse.reshape(slot_count), slot_of, axis=0).astype(jnp.float32)
    return (neighbours, log_mass)


def solution(mesh):
    placed = (P(("group", "tile"), None), P(("group", "tile")), P())
    return jax.shard_map(
        per_device,
        mesh=mesh,
        in_specs=placed,
        out_specs=(P(("group", "tile"), None), P(("group", "tile"))),
        check_vma=False,
    )
```

profile of v0, /device:TPU:1, one launch (start us, length us, event | category | flops | bytes accessed | tf_op | source)
XLA Modules:
  0.0 218.7 jit_solution(13662327656676615391)
XLA Ops:
  7.2 0.0 all-gather.2.cloned.1.call-start
  7.2 0.8 select_reduce_fusion.2
  8.1 0.2 convert_reduce_fusion
  8.3 0.7 multiply_add_fusion
  9.0 0.6 convolution_convert_fusion
  9.6 19.4 %all_to_all.22 = bf16[8,72,768]{2,1,0:T(8,128)(2,1)} all-to-all(bf16[8,72,768]{2,1,0:T(8,128)(2,1)S(1)} %bitcast.12), channel_id=1, replica_groups=mesh['group'=8,'tile'=16] {'group'}, dimensions={0} | all-to-all | bytes 1769472 | tf_op jit(solution)/shard_map/all_to_all | solution.py:58
  29.0 0.0 all-gather.2.cloned.1.call-update
  29.0 0.2 select_reduce_fusion.1
  29.2 0.7 sub.55
  29.9 4.0 %all-to-all-start = ((s32[8,1,72]{2,1,0:T(1,128)}), s32[8,1,72]{2,1,0:T(1,128)S(1)}, u32[]{:S(2)}, u32[]{:S(2)}) async-start(s32[8,1,72]{2,1,0:T(1,128)} %sub.55), calls=%async_computation | async-start | bytes 8192 | tf_op jit(solution)/shard_map/all_to_all | solution.py:65
  33.9 1.2 dynamic-slice
  35.8 2.6 %all-to-all-done = s32[8,1,72]{2,1,0:T(1,128)S(1)} async-done(((s32[8,1,72]{2,1,0:T(1,128)}), s32[8,1,72]{2,1,0:T(1,128)S(1)}, u32[]{:S(2)}, u32[]{:S(2)}) %all-to-all-start) | async-done | bytes 2336 | tf_op jit(solution)/shard_map/all_to_all | solution.py:65
  38.4 0.5 broadcast.121
  38.9 0.7 reduce.9
  39.6 0.1 reshape.184
  39.7 0.3 dynamic-update-slice
  40.0 63.1 %all-reduce = s32[9216]{0:T(1024)S(1)} all-reduce(s32[9216]{0:T(1024)S(1)} %dynamic-update-slice), channel_id=1, replica_groups=mesh['group'=8,'tile'=16] {'tile'}, use_global_device_ids=true, to_apply=%add | all-reduce | flops 9216 | bytes 73728
  103.1 25.9 %all-gather.2.cloned.1.call-done = bf16[9216,768]{1,0:T(8,128)(2,1)} async-done(((bf16[576,768]{1,0:T(8,128)(2,1)}), bf16[9216,768]{1,0:T(8,128)(2,1)}) %all-gather.2.cloned.1.call-update) | async-done | bytes 14155792 | tf_op jit(solution)/shard_map/all_gather | solution.py:82
  128.9 18.6 %select_reduce_fusion = (f32[576]{0:T(1024)S(1)}, f32[576,9216]{1,0:T(8,128)}) fusion(s32[9216]{0:T(1024)S(1)} %all-reduce, s32[576]{0:T(1024)S(1)} %iota_add_fusion, s32[576]{0:T(1024)S(1)} %reshape.184, pred[9216]{0:T(1024)(128)(4,1)S(1)} %broadcast_compare_fusion, bf16[576,768]{1,0:T(8,128)(2,1)} %bitcast.11, ...), kind=kOutput, calls=%fused_computation.3 | convolution fusion | flops 8196193792 | bytes 36327168 | tf_op jit(solution)/shard_map/dot_general | solution.py:13
  147.6 13.3 %fusion.17 = f32[576]{0:T(1024)S(1)} fusion(f32[576]{0:T(1024)S(1)} %get-tuple-element.6, s32[9216]{0:T(1024)S(1)} %all-reduce, s32[576]{0:T(1024)S(1)} %reshape.184, f32[576,9216]{1,0:T(8,128)} %get-tuple-element.7, s32[576]{0:T(1024)S(1)} %iota_add_fusion, pred[9216]{0:T(1024)(128)(4,1)S(1)} %broadcast_compare_fusion), kind=kLoop, calls=%fused_computation.46 | loop fusion | flops 47775168 | bytes 21288960 | tf_op jit(solution)/shard_map/reduce_sum | solution.py:23
  160.9 0.1 reduce_sum.42
  160.9 0.1 reduce_max.12
  161.0 0.6 copy.5
  161.6 5.0 %all-to-all-start.3 = ((bf16[8,1,72]{2,1,0:T(2,128)(2,1)}), bf16[8,1,72]{2,1,0:T(2,128)(2,1)S(1)}, u32[]{:S(2)}, u32[]{:S(2)}) async-start(bf16[8,1,72]{2,1,0:T(2,128)(2,1)} %copy.5), calls=%async_computation.3 | async-start | bytes 8192 | tf_op jit(solution)/shard_map/all_to_all | solution.py:99
  166.6 24.0 %divide_convert_fusion = bf16[576,768]{1,0:T(8,128)(2,1)} fusion(bf16[9216,768]{1,0:T(8,128)(2,1)} %all-gather.2.cloned.1.call-done, f32[576]{0:T(1024)S(1)} %get-tuple-element.5, f32[576]{0:T(1024)S(1)} %get-tuple-element.4, f32[576,9216]{1,0:T(8,128)} %get-tuple-element.7, f32[576]{0:T(1024)S(1)} %get-tuple-element.6, s32[9216]{0:T(1024)S(1)} %all-reduce, ...), kind=kOutput, calls=%fused_computation.9 | convolution fusion | flops 8202829824 | bytes 36331776 | tf_op jit(solution)/shard_map/dot_general | solution.py:24
  190.6 4.8 %all-to-all-start.2 = ((bf16[8,72,768]{2,1,0:T(8,128)(2,1)}), bf16[8,72,768]{2,1,0:T(8,128)(2,1)S(1)}, u32[]{:S(2)}, u32[]{:S(2)}) async-start(bf16[8,72,768]{2,1,0:T(8,128)(2,1)} %bitcast.3), calls=%async_computation.2 | async-start | bytes 1769472 | tf_op jit(solution)/shard_map/all_to_all | solution.py:92
  195.5 0.1 reshape.167
  195.5 1.9 gather_fusion.1
  197.4 0.6 broadcast_select_fusion.1
  198.0 10.7 %all-to-all-done.2 = bf16[8,72,768]{2,1,0:T(8,128)(2,1)S(1)} async-done(((bf16[8,72,768]{2,1,0:T(8,128)(2,1)}), bf16[8,72,768]{2,1,0:T(8,128)(2,1)S(1)}, u32[]{:S(2)}, u32[]{:S(2)}) %all-to-all-start.2) | async-done | bytes 884768 | tf_op jit(solution)/shard_map/all_to_all | solution.py:92
  208.8 2.2 gather_fusion
  210.9 0.9 broadcast_select_fusion
  (12 shorter events, 0.1 us)
Async XLA Ops:
  7.2 1.8 copy-start
  7.2 121.8 %all-gather.2.cloned.1.call-start = ((), (), s32[]{:S(2)}) async-start(), calls=%async_computation.4 | async-start | bytes 15040512 | tf_op jit(solution)/shard_map/all_gather | solution.py:82
  29.9 8.6 %all-to-all-start = ((s32[8,1,72]{2,1,0:T(1,128)}), s32[8,1,72]{2,1,0:T(1,128)S(1)}, u32[]{:S(2)}, u32[]{:S(2)}) async-start(s32[8,1,72]{2,1,0:T(1,128)} %sub.55), calls=%async_computation | async-start | bytes 8192 | tf_op jit(solution)/shard_map/all_to_all | solution.py:65
  161.6 29.0 %all-to-all-start.3 = ((bf16[8,1,72]{2,1,0:T(2,128)(2,1)}), bf16[8,1,72]{2,1,0:T(2,128)(2,1)S(1)}, u32[]{:S(2)}, u32[]{:S(2)}) async-start(bf16[8,1,72]{2,1,0:T(2,128)(2,1)} %copy.5), calls=%async_computation.3 | async-start | bytes 8192 | tf_op jit(solution)/shard_map/all_to_all | solution.py:99
  190.6 18.1 %all-to-all-start.2 = ((bf16[8,72,768]{2,1,0:T(8,128)(2,1)}), bf16[8,72,768]{2,1,0:T(8,128)(2,1)S(1)}, u32[]{:S(2)}, u32[]{:S(2)}) async-start(bf16[8,72,768]{2,1,0:T(8,128)(2,1)} %bitcast.3), calls=%async_computation.2 | async-start | bytes 1769472 | tf_op jit(solution)/shard_map/all_to_all | solution.py:92
Sparse Core Ops, SparseCore 0:
  29.1 99.7 all-gather.1
where the time goes:
time: 219 us
  blocking collectives  82.4 us (38%)
  matrix products  43.2 us (20%)
  waiting for transfers between devices  39.3 us (18%)
  other arithmetic  17.5 us (8%)
  between operations  14.8 us (7%)
  starting transfers between devices  13.8 us (6%)
  local copies, waits for them, and re-layouts  7.68 us (4%)
    unnamed x1, blocking collectives  63.1 us
    all_gather x1, waiting for transfers between devices, per_device(): key_rows = lax.all_gather(queries, 'tile', axis=0, tiled=True)  25.9 us
    dot_general x1, matrix products, partial_terms(): jnp.dot(weights.astype(jnp.bfloat16), key_rows, preferred_element_type=jn...  24 us
    all_to_all x1, blocking collectives, per_device(): lax.all_to_all(outgoing.reshape(groups_total, capacity, feature_width), '...  19.4 us
    dot_general x1, matrix products, block_scores(): lax.dot_general(queries, key_rows, (((1,), (1,)), ((), ())), preferred_el...  18.6 us
    reduce_sum x1, other arithmetic, partial_terms(): row_total = jnp.sum(weights, axis=1)  13.3 us
    all_to_all x1, waiting for transfers between devices, per_device(): lax.all_to_all(neighbour_slots.reshape(groups_total, capacity, feature_wi...  10.7 us
    all_to_all x1, starting transfers between devices, per_device(): lax.all_to_all(lse_slots.reshape(groups_total, capacity).astype(jnp.bfloa...  4.97 us
  transfers between devices with their start and end apart: 4, of which 3 were waited for; matrix products, arithmetic and copies ran while one was open for 14% of the time, Pallas kernels for 0%

commit v1 on v0

--- a/solution.py
+++ b/solution.py
@@ -6,6 +6,22 @@
 
 score_scale = 3.0
 penalty = 2.0
+
+
+def gather_around(x, axis, dim):
+    ways, here, step = (lax.axis_size(axis), lax.axis_index(axis), x.shape[dim])
+    shape = [n * ways if d == dim else n for d, n in enumerate(x.shape)]
+    full = lax.dynamic_update_slice_in_dim(jnp.zeros(shape, x.dtype), x, here * step, axis=dim)
+    going_up = going_down = x
+    for far in range(1, ways // 2 + 1):
+        going_up = lax.ppermute(going_up, axis, [(d, (d + 1) % ways) for d in range(ways)])
+        full = lax.dynamic_update_slice_in_dim(full, going_up, (here - far) % ways * step, axis=dim)
+        if 2 * far < ways:
+            going_down = lax.ppermute(going_down, axis, [(d, (d - 1) % ways) for d in range(ways)])
+            full = lax.dynamic_update_slice_in_dim(
+                full, going_down, (here + far) % ways * step, axis=dim
+            )
+    return full
 
 
 def block_scores(queries, query_ids, key_rows, key_ids):
@@ -79,7 +95,7 @@
     )
     tile_pos = lax.axis_index("tile")
     query_pos = tile_pos * slot_count + jnp.arange(slot_count, dtype=jnp.int32)
-    key_rows = lax.all_gather(queries, "tile", axis=0, tiled=True)
+    key_rows = gather_around(queries, "tile", 0)
     key_ids = lax.all_gather(query_ids, "tile", axis=0, tiled=True)
     key_pos = jnp.arange(key_rows.shape[0], dtype=jnp.int32)
     scores = block_scores(queries, query_ids, key_rows, key_ids)

time: 219 us -> 358 us (1.63)
  waiting for transfers between devices: 39.3 us -> 117 us
  starting transfers between devices: 13.8 us -> 62.6 us
  local copies, waits for them, and re-layouts: 7.68 us -> 35.9 us
  between operations: 14.8 us -> 1.47 us
    ppermute x0 -> x15, waiting for transfers between devices: none -> 103 us  [the longest x8 101 us: gather_around(): lax.ppermute(going_up, axis, [(d, (d + 1) % ways) for d in range(ways)])]
    ppermute x0 -> x15, starting transfers between devices: none -> 29.2 us  [the longest x7 26.8 us: gather_around(): lax.ppermute(going_down, axis, [(d, (d - 1) % ways) for d in range(ways)])]
    all_gather x1 -> x0, waiting for transfers between devices: 25.9 us -> none  [per_device(): key_rows = lax.all_gather(queries, 'tile', axis=0, tiled=True)]
    dynamic_update_slice x0 -> x16, local copies, waits for them, and re-layouts: none -> 20.6 us  [the longest x8 10.2 us: gather_around(): lax.dynamic_update_slice_in_dim(full, going_up, (here - far) % ways * ste...]
    all_to_all x1, starting transfers between devices: 4.97 us -> 20.2 us  [per_device(): lax.all_to_all(lse_slots.reshape(groups_total, capacity).astype(jnp.bfloa...]
    broadcast_in_dim x0 -> x1, local copies, waits for them, and re-layouts: none -> 5.85 us  [gather_around(): jnp.zeros(shape, x.dtype)]
    all_to_all x1, starting transfers between devices: 4.03 us -> 8.3 us  [per_device(): lax.all_to_all(outgoing_ids.reshape(groups_total, capacity), 'group', spl...]
  transfers between devices with their start and end apart: 4 -> 18, of which waited for: 3 -> 10; matrix products, arithmetic and copies ran while one was open for 14% -> 16% of each run, Pallas kernels for 0% -> 0%
where the time goes in v1:
time: 358 us; the launch traced here: 357 us
  waiting for transfers between devices  117 us (33%)
  blocking collectives  79.4 us (22%)
  starting transfers between devices  62.6 us (17%)
  matrix products  43.1 us (12%)
  local copies, waits for them, and re-layouts  35.9 us (10%)
  other arithmetic  17.5 us (5%)
    ppermute x8, waiting for transfers between devices, gather_around(): lax.ppermute(going_up, axis, [(d, (d + 1) % ways) for d in range(ways)])  101 us
    unnamed x1, blocking collectives  60.1 us
    ppermute x7, starting transfers between devices, gather_around(): lax.ppermute(going_down, axis, [(d, (d - 1) % ways) for d in range(ways)])  26.8 us
    dot_general x1, matrix products, partial_terms(): jnp.dot(weights.astype(jnp.bfloat16), key_rows, preferred_element_type=jn...  24 us
    all_to_all x1, starting transfers between devices, per_device(): lax.all_to_all(lse_slots.reshape(groups_total, capacity).astype(jnp.bfloa...  20.2 us
    all_to_all x1, blocking collectives, per_device(): lax.all_to_all(outgoing.reshape(groups_total, capacity, feature_width), '...  19.3 us
    dot_general x1, matrix products, block_scores(): lax.dot_general(queries, key_rows, (((1,), (1,)), ((), ())), preferred_el...  18.6 us
    reduce_sum x1, other arithmetic, partial_terms(): row_total = jnp.sum(weights, axis=1)  13.3 us
  transfers between devices with their start and end apart: 18, of which 10 were waited for; matrix products, arithmetic and copies ran while one was open for 16% of the time, Pallas kernels for 0%

profile of v1, /device:TPU:1, one launch (start us, length us, event | category | flops | bytes accessed | tf_op | source)
XLA Modules:
  0.0 357.0 jit_solution(5180012194583866021)
XLA Ops:
  3.0 19.3 %all_to_all.22 = bf16[8,72,768]{2,1,0:T(8,128)(2,1)S(1)} all-to-all(bf16[8,72,768]{2,1,0:T(8,128)(2,1)S(1)} %bitcast.14), channel_id=1, replica_groups=mesh['group'=8,'tile'=16] {'group'}, dimensions={0} | all-to-all | bytes 1769472 | tf_op jit(solution)/shard_map/all_to_all | solution.py:74
  22.3 1.6 collective-permute-start
  23.9 4.3 %collective-permute-start.1 = (bf16[576,768]{1,0:T(8,128)(2,1)S(1)}, bf16[576,768]{1,0:T(8,128)(2,1)S(1)}, u32[]{:S(2)}, u32[]{:S(2)}) collective-permute-start(bf16[576,768]{1,0:T(8,128)(2,1)S(1)} %bitcast.11), channel_id=1, source_target_pairs={{0,15},{1,0},{2,1},{3,2},{4,3},{5,4},{6,5},{7,6},{8,7},{9,8},{10,9... | collective-permute-start | bytes 2654216 | tf_op jit(solution)/shard_map/ppermute | solution.py:20
  28.2 19.2 %collective-permute-done = bf16[576,768]{1,0:T(8,128)(2,1)S(1)} collective-permute-done((bf16[576,768]{1,0:T(8,128)(2,1)S(1)}, bf16[576,768]{1,0:T(8,128)(2,1)S(1)}, u32[]{:S(2)}, u32[]{:S(2)}) %collective-permute-start) | collective-permute-done | bytes 884768 | tf_op jit(solution)/shard_map/ppermute | solution.py:17
  47.4 4.8 %collective-permute-start.3 = (bf16[576,768]{1,0:T(8,128)(2,1)S(1)}, bf16[576,768]{1,0:T(8,128)(2,1)S(1)}, u32[]{:S(2)}, u32[]{:S(2)}) collective-permute-start(bf16[576,768]{1,0:T(8,128)(2,1)S(1)} %collective-permute-done.1), channel_id=1, source_target_pairs={{0,15},{1,0},{2,1},{3,2},{4,3},{5,4},{6,5},{7,6},{8,7},{9,8},{10,9... | collective-permute-start | bytes 2654216 | tf_op jit(solution)/shard_map/ppermute | solution.py:20
  52.2 18.3 %collective-permute-done.2 = bf16[576,768]{1,0:T(8,128)(2,1)S(1)} collective-permute-done((bf16[576,768]{1,0:T(8,128)(2,1)S(1)}, bf16[576,768]{1,0:T(8,128)(2,1)S(1)}, u32[]{:S(2)}, u32[]{:S(2)}) %collective-permute-start.2) | collective-permute-done | bytes 884768 | tf_op jit(solution)/shard_map/ppermute | solution.py:17
  71.4 4.0 %collective-permute-start.5 = (bf16[576,768]{1,0:T(8,128)(2,1)S(1)}, bf16[576,768]{1,0:T(8,128)(2,1)S(1)}, u32[]{:S(2)}, u32[]{:S(2)}) collective-permute-start(bf16[576,768]{1,0:T(8,128)(2,1)S(1)} %collective-permute-done.3), channel_id=1, source_target_pairs={{0,15},{1,0},{2,1},{3,2},{4,3},{5,4},{6,5},{7,6},{8,7},{9,8},{10,9... | collective-permute-start | bytes 2654216 | tf_op jit(solution)/shard_map/ppermute | solution.py:20
  75.4 17.3 %collective-permute-done.4 = bf16[576,768]{1,0:T(8,128)(2,1)S(1)} collective-permute-done((bf16[576,768]{1,0:T(8,128)(2,1)S(1)}, bf16[576,768]{1,0:T(8,128)(2,1)S(1)}, u32[]{:S(2)}, u32[]{:S(2)}) %collective-permute-start.4) | collective-permute-done | bytes 884768 | tf_op jit(solution)/shard_map/ppermute | solution.py:17
  92.7 4.8 %collective-permute-start.7 = (bf16[576,768]{1,0:T(8,128)(2,1)S(1)}, bf16[576,768]{1,0:T(8,128)(2,1)}, u32[]{:S(2)}, u32[]{:S(2)}) collective-permute-start(bf16[576,768]{1,0:T(8,128)(2,1)S(1)} %collective-permute-done.5), channel_id=1, source_target_pairs={{0,15},{1,0},{2,1},{3,2},{4,3},{5,4},{6,5},{7,6},{8,7},{9,8},{10,9... | collective-permute-start | bytes 2654216 | tf_op jit(solution)/shard_map/ppermute | solution.py:20
  97.4 16.4 %collective-permute-done.6 = bf16[576,768]{1,0:T(8,128)(2,1)S(1)} collective-permute-done((bf16[576,768]{1,0:T(8,128)(2,1)S(1)}, bf16[576,768]{1,0:T(8,128)(2,1)S(1)}, u32[]{:S(2)}, u32[]{:S(2)}) %collective-permute-start.6) | collective-permute-done | bytes 884768 | tf_op jit(solution)/shard_map/ppermute | solution.py:17
  114.8 4.8 %collective-permute-start.9 = (bf16[576,768]{1,0:T(8,128)(2,1)}, bf16[576,768]{1,0:T(8,128)(2,1)}, u32[]{:S(2)}, u32[]{:S(2)}) collective-permute-start(bf16[576,768]{1,0:T(8,128)(2,1)} %collective-permute-done.7), channel_id=1, source_target_pairs={{0,15},{1,0},{2,1},{3,2},{4,3},{5,4},{6,5},{7,6},{8,7},{9,8},{10,9... | collective-permute-start | bytes 2654216 | tf_op jit(solution)/shard_map/ppermute | solution.py:20
  119.8 15.4 %collective-permute-done.8 = bf16[576,768]{1,0:T(8,128)(2,1)} collective-permute-done((bf16[576,768]{1,0:T(8,128)(2,1)S(1)}, bf16[576,768]{1,0:T(8,128)(2,1)}, u32[]{:S(2)}, u32[]{:S(2)}) %collective-permute-start.8) | collective-permute-done | bytes 884768 | tf_op jit(solution)/shard_map/ppermute | solution.py:17
  135.9 8.3 %all-to-all-start = ((s32[8,1,72]{2,1,0:T(1,128)}), s32[8,1,72]{2,1,0:T(1,128)S(1)}, u32[]{:S(2)}, u32[]{:S(2)}) async-start(s32[8,1,72]{2,1,0:T(1,128)} %sub.79), calls=%async_computation | async-start | bytes 8192 | tf_op jit(solution)/shard_map/all_to_all | solution.py:81
  146.1 3.0 all-to-all-done
  150.7 60.1 %all-reduce = s32[9216]{0:T(1024)S(1)} all-reduce(s32[9216]{0:T(1024)S(1)} %dynamic-update-slice), channel_id=1, replica_groups=mesh['group'=8,'tile'=16] {'tile'}, use_global_device_ids=true, to_apply=%add | all-reduce | flops 9216 | bytes 73728
  210.9 5.9 %broadcast_in_dim.75 = bf16[9216,768]{1,0:T(8,128)(2,1)} broadcast(bf16[]{:T(256)} %constant.131.clone.1), dimensions={} | broadcast | bytes 14155778 | tf_op jit(solution)/shard_map/broadcast_in_dim | solution.py:14
  224.4 4.1 %collective-permute-start.13 = (bf16[576,768]{1,0:T(8,128)(2,1)S(1)}, bf16[576,768]{1,0:T(8,128)(2,1)S(1)}, u32[]{:S(2)}, u32[]{:S(2)}) collective-permute-start(bf16[576,768]{1,0:T(8,128)(2,1)S(1)} %collective-permute-done.11), channel_id=1, source_target_pairs={{0,15},{1,0},{2,1},{3,2},{4,3},{5,4},{6,5},{7,6},{8,7},{9,8},{10,9... | collective-permute-start | bytes 2654216 | tf_op jit(solution)/shard_map/ppermute | solution.py:20
  229.5 3.7 %collective-permute-done.12 = bf16[576,768]{1,0:T(8,128)(2,1)S(1)} collective-permute-done((bf16[576,768]{1,0:T(8,128)(2,1)}, bf16[576,768]{1,0:T(8,128)(2,1)S(1)}, u32[]{:S(2)}, u32[]{:S(2)}) %collective-permute-start.12) | collective-permute-done | bytes 884768 | tf_op jit(solution)/shard_map/ppermute | solution.py:17
  233.2 2.2 constant_dynamic-update-slice_fusion.7
  235.4 2.2 constant_dynamic-update-slice_fusion.6
  237.6 2.2 constant_dynamic-update-slice_fusion.5
  239.8 2.1 constant_dynamic-update-slice_fusion.4
  243.9 1.9 collective-permute-done.13
  246.8 11.1 %collective-permute-done.14 = bf16[576,768]{1,0:T(8,128)(2,1)S(1)} collective-permute-done((bf16[576,768]{1,0:T(8,128)(2,1)S(1)}, bf16[576,768]{1,0:T(8,128)(2,1)S(1)}, u32[]{:S(2)}, u32[]{:S(2)}) %collective-permute-start.14) | collective-permute-done | bytes 884768 | tf_op jit(solution)/shard_map/ppermute | solution.py:17
  258.9 18.6 %select_reduce_fusion = (f32[576]{0:T(1024)S(1)}, f32[576,9216]{1,0:T(8,128)}) fusion(s32[9216]{0:T(1024)S(1)} %all-reduce, s32[576]{0:T(1024)S(1)} %iota_add_fusion, s32[576]{0:T(1024)S(1)} %reshape.184, pred[9216]{0:T(1024)(128)(4,1)S(1)} %broadcast_compare_fusion, bf16[576,768]{1,0:T(8,128)(2,1)S(1)} %bitcast.13, ...), kind=kOutput, calls=%fused_computation.3 | convolution fusion | flops 8196193792 | bytes 36327168 | tf_op jit(solution)/shard_map/dot_general | solution.py:29
  277.4 13.3 %fusion.17 = f32[576]{0:T(1024)S(1)} fusion(f32[576]{0:T(1024)S(1)} %get-tuple-element.6, s32[9216]{0:T(1024)S(1)} %all-reduce, s32[576]{0:T(1024)S(1)} %reshape.184, f32[576,9216]{1,0:T(8,128)} %get-tuple-element.7, s32[576]{0:T(1024)S(1)} %iota_add_fusion, pred[9216]{0:T(1024)(128)(4,1)S(1)} %broadcast_compare_fusion), kind=kLoop, calls=%fused_computation.62 | loop fusion | flops 47775168 | bytes 21288960 | tf_op jit(solution)/shard_map/reduce_sum | solution.py:39
  291.5 20.2 %all-to-all-start.3 = ((bf16[8,1,72]{2,1,0:T(2,128)(2,1)}), bf16[8,1,72]{2,1,0:T(2,128)(2,1)S(1)}, u32[]{:S(2)}, u32[]{:S(2)}) async-start(bf16[8,1,72]{2,1,0:T(2,128)(2,1)} %copy.5), calls=%async_computation.3 | async-start | bytes 8192 | tf_op jit(solution)/shard_map/all_to_all | solution.py:115
  311.8 24.0 %divide_convert_fusion = bf16[576,768]{1,0:T(8,128)(2,1)} fusion(bf16[9216,768]{1,0:T(8,128)(2,1)} %constant_dynamic-update-slice_fusion, f32[576]{0:T(1024)S(1)} %get-tuple-element.5, f32[576]{0:T(1024)S(1)} %get-tuple-element.4, f32[576,9216]{1,0:T(8,128)} %get-tuple-element.7, f32[576]{0:T(1024)S(1)} %get-tuple-element.6, s32[9216]{0:T(1024)S(1)} %all-reduce, ...), kind=kOutput, calls=%fused_computation.9 | convolution fusion | flops 8202829824 | bytes 36331776 | tf_op jit(solution)/shard_map/dot_general | solution.py:40
  335.7 4.8 %all-to-all-start.2 = ((bf16[8,72,768]{2,1,0:T(8,128)(2,1)}), bf16[8,72,768]{2,1,0:T(8,128)(2,1)S(1)}, u32[]{:S(2)}, u32[]{:S(2)}) async-start(bf16[8,72,768]{2,1,0:T(8,128)(2,1)} %bitcast.3), calls=%async_computation.2 | async-start | bytes 1769472 | tf_op jit(solution)/shard_map/all_to_all | solution.py:108
  340.7 1.9 gather_fusion.1
  343.2 10.7 %all-to-all-done.2 = bf16[8,72,768]{2,1,0:T(8,128)(2,1)S(1)} async-done(((bf16[8,72,768]{2,1,0:T(8,128)(2,1)}), bf16[8,72,768]{2,1,0:T(8,128)(2,1)S(1)}, u32[]{:S(2)}, u32[]{:S(2)}) %all-to-all-start.2) | async-done | bytes 884768 | tf_op jit(solution)/shard_map/all_to_all | solution.py:108
  353.9 2.2 gather_fusion
  (76 shorter events, 23.0 us)
Async XLA Ops:
  0.6 1.8 copy-start
  22.3 25.2 %collective-permute-start = (bf16[576,768]{1,0:T(8,128)(2,1)S(1)}, bf16[576,768]{1,0:T(8,128)(2,1)S(1)}, u32[]{:S(2)}, u32[]{:S(2)}) collective-permute-start(bf16[576,768]{1,0:T(8,128)(2,1)S(1)} %bitcast.10), channel_id=1, source_target_pairs={{0,1},{1,2},{2,3},{3,4},{4,5},{5,6},{6,7},{7,8},{8,9},{9,10},{10,1... | collective-permute-start | bytes 2654216 | tf_op jit(solution)/shard_map/ppermute | solution.py:17
  23.9 23.5 %collective-permute-start.1 = (bf16[576,768]{1,0:T(8,128)(2,1)S(1)}, bf16[576,768]{1,0:T(8,128)(2,1)S(1)}, u32[]{:S(2)}, u32[]{:S(2)}) collective-permute-start(bf16[576,768]{1,0:T(8,128)(2,1)S(1)} %bitcast.11), channel_id=1, source_target_pairs={{0,15},{1,0},{2,1},{3,2},{4,3},{5,4},{6,5},{7,6},{8,7},{9,8},{10,9... | collective-permute-start | bytes 2654216 | tf_op jit(solution)/shard_map/ppermute | solution.py:20
  47.4 23.1 %collective-permute-start.2 = (bf16[576,768]{1,0:T(8,128)(2,1)S(1)}, bf16[576,768]{1,0:T(8,128)(2,1)S(1)}, u32[]{:S(2)}, u32[]{:S(2)}) collective-permute-start(bf16[576,768]{1,0:T(8,128)(2,1)S(1)} %collective-permute-done), channel_id=1, source_target_pairs={{0,1},{1,2},{2,3},{3,4},{4,5},{5,6},{6,7},{7,8},{8,9},{9,10},{10,1... | collective-permute-start | bytes 2654216 | tf_op jit(solution)/shard_map/ppermute | solution.py:17
  47.4 23.1 %collective-permute-start.3 = (bf16[576,768]{1,0:T(8,128)(2,1)S(1)}, bf16[576,768]{1,0:T(8,128)(2,1)S(1)}, u32[]{:S(2)}, u32[]{:S(2)}) collective-permute-start(bf16[576,768]{1,0:T(8,128)(2,1)S(1)} %collective-permute-done.1), channel_id=1, source_target_pairs={{0,15},{1,0},{2,1},{3,2},{4,3},{5,4},{6,5},{7,6},{8,7},{9,8},{10,9... | collective-permute-start | bytes 2654216 | tf_op jit(solution)/shard_map/ppermute | solution.py:20
  70.5 0.9 copy-start.1
  70.5 22.1 %collective-permute-start.4 = (bf16[576,768]{1,0:T(8,128)(2,1)S(1)}, bf16[576,768]{1,0:T(8,128)(2,1)S(1)}, u32[]{:S(2)}, u32[]{:S(2)}) collective-permute-start(bf16[576,768]{1,0:T(8,128)(2,1)S(1)} %collective-permute-done.2), channel_id=1, source_target_pairs={{0,1},{1,2},{2,3},{3,4},{4,5},{5,6},{6,7},{7,8},{8,9},{9,10},{10,1... | collective-permute-start | bytes 2654216 | tf_op jit(solution)/shard_map/ppermute | solution.py:17
  71.4 21.2 %copy-start.3 = (bf16[576,768]{1,0:T(8,128)(2,1)}, bf16[576,768]{1,0:T(8,128)(2,1)S(1)}, u32[]{:S(2)}) copy-start(bf16[576,768]{1,0:T(8,128)(2,1)S(1)} %collective-permute-done.3) | copy-start | bytes 2654212
  71.4 21.2 %collective-permute-start.5 = (bf16[576,768]{1,0:T(8,128)(2,1)S(1)}, bf16[576,768]{1,0:T(8,128)(2,1)S(1)}, u32[]{:S(2)}, u32[]{:S(2)}) collective-permute-start(bf16[576,768]{1,0:T(8,128)(2,1)S(1)} %collective-permute-done.3), channel_id=1, source_target_pairs={{0,15},{1,0},{2,1},{3,2},{4,3},{5,4},{6,5},{7,6},{8,7},{9,8},{10,9... | collective-permute-start | bytes 2654216 | tf_op jit(solution)/shard_map/ppermute | solution.py:20
  92.6 22.1 %copy-start.7 = (bf16[576,768]{1,0:T(8,128)(2,1)}, bf16[576,768]{1,0:T(8,128)(2,1)S(1)}, u32[]{:S(2)}) copy-start(bf16[576,768]{1,0:T(8,128)(2,1)S(1)} %collective-permute-done.4) | copy-start | bytes 2654212
  92.6 21.2 %collective-permute-start.6 = (bf16[576,768]{1,0:T(8,128)(2,1)S(1)}, bf16[576,768]{1,0:T(8,128)(2,1)S(1)}, u32[]{:S(2)}, u32[]{:S(2)}) collective-permute-start(bf16[576,768]{1,0:T(8,128)(2,1)S(1)} %collective-permute-done.4), channel_id=1, source_target_pairs={{0,1},{1,2},{2,3},{3,4},{4,5},{5,6},{6,7},{7,8},{8,9},{9,10},{10,1... | collective-permute-start | bytes 2654216 | tf_op jit(solution)/shard_map/ppermute | solution.py:17
  92.7 22.1 %copy-start.9 = (bf16[576,768]{1,0:T(8,128)(2,1)}, bf16[576,768]{1,0:T(8,128)(2,1)S(1)}, u32[]{:S(2)}) copy-start(bf16[576,768]{1,0:T(8,128)(2,1)S(1)} %collective-permute-done.5) | copy-start | bytes 2654212
  92.7 22.1 %collective-permute-start.7 = (bf16[576,768]{1,0:T(8,128)(2,1)S(1)}, bf16[576,768]{1,0:T(8,128)(2,1)}, u32[]{:S(2)}, u32[]{:S(2)}) collective-permute-start(bf16[576,768]{1,0:T(8,128)(2,1)S(1)} %collective-permute-done.5), channel_id=1, source_target_pairs={{0,15},{1,0},{2,1},{3,2},{4,3},{5,4},{6,5},{7,6},{8,7},{9,8},{10,9... | collective-permute-start | bytes 2654216 | tf_op jit(solution)/shard_map/ppermute | solution.py:20
  113.9 0.9 copy-start.5
  114.8 20.4 %collective-permute-start.8 = (bf16[576,768]{1,0:T(8,128)(2,1)S(1)}, bf16[576,768]{1,0:T(8,128)(2,1)}, u32[]{:S(2)}, u32[]{:S(2)}) collective-permute-start(bf16[576,768]{1,0:T(8,128)(2,1)S(1)} %collective-permute-done.6), channel_id=1, source_target_pairs={{0,1},{1,2},{2,3},{3,4},{4,5},{5,6},{6,7},{7,8},{8,9},{9,10},{10,1... | collective-permute-start | bytes 2654216 | tf_op jit(solution)/shard_map/ppermute | solution.py:17
  114.8 96.0 %collective-permute-start.9 = (bf16[576,768]{1,0:T(8,128)(2,1)}, bf16[576,768]{1,0:T(8,128)(2,1)}, u32[]{:S(2)}, u32[]{:S(2)}) collective-permute-start(bf16[576,768]{1,0:T(8,128)(2,1)} %collective-permute-done.7), channel_id=1, source_target_pairs={{0,15},{1,0},{2,1},{3,2},{4,3},{5,4},{6,5},{7,6},{8,7},{9,8},{10,9... | collective-permute-start | bytes 2654216 | tf_op jit(solution)/shard_map/ppermute | solution.py:20
  135.2 82.6 %collective-permute-start.10 = (bf16[576,768]{1,0:T(8,128)(2,1)}, bf16[576,768]{1,0:T(8,128)(2,1)}, u32[]{:S(2)}, u32[]{:S(2)}) collective-permute-start(bf16[576,768]{1,0:T(8,128)(2,1)} %collective-permute-done.8), channel_id=1, source_target_pairs={{0,1},{1,2},{2,3},{3,4},{4,5},{5,6},{6,7},{7,8},{8,9},{9,10},{10,1... | collective-permute-start | bytes 2654216 | tf_op jit(solution)/shard_map/ppermute | solution.py:17
  135.9 13.2 %all-to-all-start = ((s32[8,1,72]{2,1,0:T(1,128)}), s32[8,1,72]{2,1,0:T(1,128)S(1)}, u32[]{:S(2)}, u32[]{:S(2)}) async-start(s32[8,1,72]{2,1,0:T(1,128)} %sub.79), calls=%async_computation | async-start | bytes 8192 | tf_op jit(solution)/shard_map/all_to_all | solution.py:81
  210.8 9.7 %copy-start.2 = (bf16[576,768]{1,0:T(8,128)(2,1)S(1)}, bf16[576,768]{1,0:T(8,128)(2,1)}, u32[]{:S(2)}) copy-start(bf16[576,768]{1,0:T(8,128)(2,1)} %copy-done.1) | copy-start | bytes 2654212
  210.8 10.7 %copy-start.4 = (bf16[576,768]{1,0:T(8,128)(2,1)S(1)}, bf16[576,768]{1,0:T(8,128)(2,1)}, u32[]{:S(2)}) copy-start(bf16[576,768]{1,0:T(8,128)(2,1)} %copy-done.3) | copy-start | bytes 2654212
  210.8 11.7 %copy-start.8 = (bf16[576,768]{1,0:T(8,128)(2,1)S(1)}, bf16[576,768]{1,0:T(8,128)(2,1)}, u32[]{:S(2)}) copy-start(bf16[576,768]{1,0:T(8,128)(2,1)} %copy-done.7) | copy-start | bytes 2654212
  210.8 12.6 %copy-start.10 = (bf16[576,768]{1,0:T(8,128)(2,1)S(1)}, bf16[576,768]{1,0:T(8,128)(2,1)}, u32[]{:S(2)}) copy-start(bf16[576,768]{1,0:T(8,128)(2,1)} %copy-done.9) | copy-start | bytes 2654212
  210.8 17.7 %copy-start.6 = (bf16[576,768]{1,0:T(8,128)(2,1)S(1)}, bf16[576,768]{1,0:T(8,128)(2,1)}, u32[]{:S(2)}) copy-start(bf16[576,768]{1,0:T(8,128)(2,1)} %copy-done.5) | copy-start | bytes 2654212
  210.8 13.6 %collective-permute-start.11 = (bf16[576,768]{1,0:T(8,128)(2,1)}, bf16[576,768]{1,0:T(8,128)(2,1)S(1)}, u32[]{:S(2)}, u32[]{:S(2)}) collective-permute-start(bf16[576,768]{1,0:T(8,128)(2,1)} %collective-permute-done.9), channel_id=1, source_target_pairs={{0,15},{1,0},{2,1},{3,2},{4,3},{5,4},{6,5},{7,6},{8,7},{9,8},{10,9... | collective-permute-start | bytes 2654216 | tf_op jit(solution)/shard_map/ppermute | solution.py:20
  217.7 15.5 %collective-permute-start.12 = (bf16[576,768]{1,0:T(8,128)(2,1)}, bf16[576,768]{1,0:T(8,128)(2,1)S(1)}, u32[]{:S(2)}, u32[]{:S(2)}) collective-permute-start(bf16[576,768]{1,0:T(8,128)(2,1)} %collective-permute-done.10), channel_id=1, source_target_pairs={{0,1},{1,2},{2,3},{3,4},{4,5},{5,6},{6,7},{7,8},{8,9},{9,10},{10,1... | collective-permute-start | bytes 2654216 | tf_op jit(solution)/shard_map/ppermute | solution.py:17
  224.4 21.4 %collective-permute-start.13 = (bf16[576,768]{1,0:T(8,128)(2,1)S(1)}, bf16[576,768]{1,0:T(8,128)(2,1)S(1)}, u32[]{:S(2)}, u32[]{:S(2)}) collective-permute-start(bf16[576,768]{1,0:T(8,128)(2,1)S(1)} %collective-permute-done.11), channel_id=1, source_target_pairs={{0,15},{1,0},{2,1},{3,2},{4,3},{5,4},{6,5},{7,6},{8,7},{9,8},{10,9... | collective-permute-start | bytes 2654216 | tf_op jit(solution)/shard_map/ppermute | solution.py:20
  233.2 24.7 %collective-permute-start.14 = (bf16[576,768]{1,0:T(8,128)(2,1)S(1)}, bf16[576,768]{1,0:T(8,128)(2,1)S(1)}, u32[]{:S(2)}, u32[]{:S(2)}) collective-permute-start(bf16[576,768]{1,0:T(8,128)(2,1)S(1)} %collective-permute-done.12), channel_id=1, source_target_pairs={{0,1},{1,2},{2,3},{3,4},{4,5},{5,6},{6,7},{7,8},{8,9},{9,10},{10,1... | collective-permute-start | bytes 2654216 | tf_op jit(solution)/shard_map/ppermute | solution.py:17
  291.5 44.2 %all-to-all-start.3 = ((bf16[8,1,72]{2,1,0:T(2,128)(2,1)}), bf16[8,1,72]{2,1,0:T(2,128)(2,1)S(1)}, u32[]{:S(2)}, u32[]{:S(2)}) async-start(bf16[8,1,72]{2,1,0:T(2,128)(2,1)} %copy.5), calls=%async_computation.3 | async-start | bytes 8192 | tf_op jit(solution)/shard_map/all_to_all | solution.py:115
  335.7 18.2 %all-to-all-start.2 = ((bf16[8,72,768]{2,1,0:T(8,128)(2,1)}), bf16[8,72,768]{2,1,0:T(8,128)(2,1)S(1)}, u32[]{:S(2)}, u32[]{:S(2)}) async-start(bf16[8,72,768]{2,1,0:T(8,128)(2,1)} %bitcast.3), calls=%async_computation.2 | async-start | bytes 1769472 | tf_op jit(solution)/shard_map/all_to_all | solution.py:108
